TPU v7x, 32 devices: a whole 2x2x4 slice. The times are simulated.
32 devices in a mesh: cluster: 4 (over z), tm: 8 (over y, x, core).
Axes of the slice: x: 2, y: 2, z: 4, core: 2. Of those that a mesh axis runs over, the one named last changes fastest.
Arguments:
- obs: float32 [12, 512, 128], P('cluster', 'tm'), parts along dimension 0, may hold values from -6 to 6
- present: int32 [12, 512], P('cluster', 'tm'), parts along dimension 0, may hold values 0 or 1
- sensors: int32 [4], P('cluster'), parts along dimension 0, may hold values from 32 to 128
- log_prec: float32 [512], P('cluster'), parts along dimension 0, may hold values from -1 to 1
- dynamics: float32 [512, 128], P('cluster'), parts along dimension 0, may hold values from -1 to 1
- prior_var: float32 [512], P('cluster'), parts along dimension 0, may hold values from 0 to 0.06, as said below
- obs_map: float32 [512, 128], P('cluster'), parts along dimension 0, may hold values from -0.5 to 0.5
- init_state: float32 [12, 128], P('cluster'), parts along dimension 0, may hold values from -6 to 6
Outputs:
- smoothed: float32 [12, 512, 128], P('cluster', 'tm'), parts along dimension 0
- new_log_prec: float32 [512], P('cluster'), parts along dimension 0
- mean_loglik: float32 [4], P('cluster'), parts along dimension 0
There are 4 independent parts, one for each index of `cluster`. A program takes and returns all parts, laid end to end along the dimension named above; each array names one. Nothing has to cross between parts.
Inputs may be any that keep to these rules, and one draw needn't show every extreme that they name: `prior_var`: positive variances.
All inputs are finite; a program needn't handle non-finite values. No bound on the sum of `present` on one device may be relied on, other than what follows from the above.
Results may differ from a plain program's by a relative error of at most 0.0003.
Values sent between devices are 32-bit elements; how exact they have to be, the bound alone decides.
A program may use at most 128 MiB of HBM per device.

v0:
```python
import functools
import math

import jax
import jax.numpy as jnp
from jax import lax
from jax.experimental import pallas as pl
from jax.experimental.pallas import tpu as pltpu
from jax.sharding import PartitionSpec as P

F32 = jnp.float32
BF16 = jnp.bfloat16
MESH = pl.DeviceIdType.MESH
WORD = 4


def stacked(a):
    high = a.astype(BF16).astype(F32)
    return jnp.concatenate([high, a - high], axis=0).astype(BF16)


def twice(s):
    return jnp.concatenate([s, s], axis=1)


def product(left, right):
    full = jnp.dot(left, right, preferred_element_type=F32)
    rows = full.shape[0] // 2
    return full[:rows] + full[rows:]


def times(a, right):
    return product(twice(stacked(a)), right)


def over(count, width, body):
    if count <= width:
        for i in range(count):
            body(i)
        return
    assert count % width == 0

    def step(lap, _):
        for i in range(width):
            body(lap * width + i)
        return 0

    lax.fori_loop(0, count // width, step, 0)


def kernel(
    n, seqs, steps,
    present_s, sensors_s, obs, present_v, log_prec, dyn, prior_var, obs_map, init,
    out, new_prec, loglik,
    words, table, nodes, vecs, ents, pair_rhs, step_rhs, drive, mask, offs, prior, filt,
    suffix, chunk8, in_buf, out_buf, off_buf, off_in, sum_buf, sum_in,
    chain_sem, off_send, off_recv, sum_send, sum_recv,
):
    pos = lax.axis_index("tm")
    states = dyn.shape[0]
    chunks = steps // WORD
    total = seqs * chunks
    levels = int(math.log2(chunks))
    first = [0]
    for level in range(1, levels + 1):
        first.append(first[-1] + (total >> (level - 1) if level > 1 else 0))

    in_buf[...] = jnp.zeros_like(in_buf)
    off_in[...] = jnp.zeros_like(off_in)
    barrier = pltpu.get_barrier_semaphore()
    for d in range(1, n):
        pl.semaphore_signal(barrier, inc=1, device_id={"tm": lax.rem(pos + d, n)}, device_id_type=MESH)

    lane = lax.broadcasted_iota(jnp.int32, (1, states), 1)
    active = (lane < sensors_s[0]).astype(F32)
    weight = jnp.exp(log_prec[...])
    weight_on = weight * active
    pv = prior_var[...]
    d_mat = dyn[...]
    d_t = d_mat.T
    h_mat = obs_map[...]
    h_rhs = stacked(h_mat)
    d_rhs = stacked(d_mat)
    readout = times(h_mat, d_rhs).T
    f_t = d_t - times(readout * weight_on, h_rhs) * pv

    for b in range(seqs):
        def word(k, b=b):
            t = k * WORD
            w = present_s[b, t]
            for i in range(1, WORD):
                w = w * 2 + present_s[b, t + i]
            words[b * chunks + k] = w
        over(chunks, 16, word)
        row = jnp.broadcast_to(present_v[b : b + 1, :].astype(F32), (steps, steps))
        same = lax.broadcasted_iota(jnp.int32, (steps, steps), 0) == lax.broadcasted_iota(jnp.int32, (steps, steps), 1)
        column = jnp.sum(jnp.where(same, row, 0.0), axis=1, keepdims=True)
        mask[b * steps : (b + 1) * steps, :] = jnp.broadcast_to(column, (steps, states))

    drive[...] = times(obs[...] * weight_on, h_rhs) * pv * mask[...]

    both = jnp.concatenate([d_t, f_t], axis=1)
    step_rhs[...] = stacked(both)
    pairs = []
    for a in (d_t, f_t):
        pairs.append(times(a, step_rhs[...]))
    pair_rhs[...] = stacked(jnp.concatenate(pairs, axis=1))
    for a in range(4):
        rows = pairs[a // 2][:, (a % 2) * states : (a % 2 + 1) * states]
        quad = times(rows, pair_rhs[...])
        for c in range(4):
            table[a * 4 + c] = stacked(quad[:, c * states : (c + 1) * states])

    def at(ref, i):
        return ref[pl.ds(i, total, stride=WORD), :]

    def advance(x, i):
        y = times(x, step_rhs[...])
        return jnp.where(at(mask, i) > 0.5, y[:, states:], y[:, :states]) + at(drive, i)

    x = at(drive, 0)
    for i in range(1, WORD):
        x = advance(x, i)
    offs[...] = x

    eye = (
        lax.broadcasted_iota(jnp.int32, (states, states), 0)
        == lax.broadcasted_iota(jnp.int32, (states, states), 1)
    ).astype(F32)
    residual = eye - jnp.dot(d_t, d_mat, precision=lax.Precision.HIGHEST, preferred_element_type=F32)
    by_one = times(jnp.concatenate([residual, d_mat], axis=0), d_rhs)
    r_1, d_2 = by_one[:states], by_one[states:]
    by_two = times(jnp.concatenate([residual, r_1, d_mat, d_2], axis=0), stacked(d_2))
    r_2, r_3 = by_two[:states], by_two[states : 2 * states]
    d_3, d_4 = by_two[2 * states : 3 * states], by_two[3 * states :]
    tail_rhs = stacked(jnp.concatenate([residual, r_1, r_2, r_3], axis=1))
    fill_rhs = stacked(jnp.concatenate([d_4, d_3, d_2, d_mat], axis=1))
    power = stacked(d_4)
    powers = [power]

    for level in range(1, levels + 1):
        base, below = first[level], first[level - 1]

        def compose(j, level=level, base=base, below=below):
            if level == 1:
                left, right = table[words[2 * j]], table[words[2 * j + 1]]
                v_left, v_right = offs[pl.ds(2 * j, 1), :], offs[pl.ds(2 * j + 1, 1), :]
            else:
                left, right = nodes[below + 2 * j], nodes[below + 2 * j + 1]
                v_left, v_right = vecs[pl.ds(below + 2 * j, 1), :], vecs[pl.ds(below + 2 * j + 1, 1), :]
            rows = jnp.concatenate([left, stacked(jnp.broadcast_to(v_left, (8, states)))], axis=0)
            y = jnp.dot(twice(rows), right, preferred_element_type=F32)
            nodes[base + j] = stacked(y[:states] + y[states : 2 * states])
            vecs[pl.ds(base + j, 1), :] = (
                y[2 * states : 2 * states + 1] + y[2 * states + 8 : 2 * states + 9] + v_right
            )

        over(total >> level, 6, compose)
        power = stacked(product(twice(powers[-1]), powers[-1]))
        powers.append(power)
    laps = []
    for _ in range(int(math.log2(n))):
        laps.append(power)
        power = stacked(product(twice(power), power))

    pl.semaphore_wait(barrier, n - 1)
    row8 = lax.broadcasted_iota(jnp.int32, (8, states), 0)

    chain = pltpu.make_async_remote_copy(
        src_ref=out_buf, dst_ref=in_buf, send_sem=chain_sem.at[0], recv_sem=chain_sem.at[1],
        device_id={"tm": lax.rem(pos + 1, n)}, device_id_type=MESH,
    )

    @pl.when(pos == 0)
    def _():
        in_buf[0:seqs, :] = init[...]

    @pl.when(pos > 0)
    def _():
        chain.wait_recv()

    entering = in_buf[...]
    top = first[levels]
    left = twice(stacked(entering))

    @pl.when(pos < n - 1)
    def _():
        leaving = jnp.zeros((8, states), F32)
        for b in range(seqs):
            y = product(left, nodes[top + b]) + vecs[top + b : top + b + 1, :]
            leaving = jnp.where(row8 == b, y, leaving)
        out_buf[...] = leaving
        chain.start()

    e_first = [0]
    for level in range(levels, 0, -1):
        e_first.append(e_first[-1] + (((total >> level) + 7) // 8) * 8)
    ents[0:seqs, :] = entering[0:seqs]
    for lap, level in enumerate(range(levels, 0, -1)):
        source, target, below = e_first[lap], e_first[lap + 1], first[level - 1]

        def descend(j, level=level, source=source, target=target, below=below):
            e = ents[pl.ds(source + j, 1), :]
            if level == 1:
                mat, v = table[words[2 * j]], offs[pl.ds(2 * j, 1), :]
            else:
                mat, v = nodes[below + 2 * j], vecs[pl.ds(below + 2 * j, 1), :]
            y = times(jnp.broadcast_to(e, (8, states)), mat)
            ents[pl.ds(target + 2 * j, 1), :] = e
            ents[pl.ds(target + 2 * j + 1, 1), :] = y[0:1] + v

        over(total >> level, 6, descend)

    x = ents[pl.ds(e_first[-1], total), :]
    for i in range(WORD):
        prior[i * total : (i + 1) * total, :] = x
        x = advance(x, i)
        filt[i * total : (i + 1) * total, :] = x

    y = times(filt[...], tail_rhs)

    def part(i, k):
        return y[i * total : (i + 1) * total, k * states : (k + 1) * states]

    chunk8[...] = jnp.zeros_like(chunk8)
    for i in range(WORD):
        z = part(i, 0)
        for j in range(i + 1, WORD):
            z = z + part(j, j - i)
        suffix[i * total : (i + 1) * total, :] = z
        if i == 0:
            for b in range(seqs):
                chunk8[pl.ds(b, chunks, stride=8), :] = z[b * chunks : (b + 1) * chunks]

    ups = [chunk8[...].reshape(chunks, 8, states)]
    for level in range(levels):
        pair = ups[-1].reshape(ups[-1].shape[0] // 2, 2, 8, states)
        half = pair.shape[0]
        later = times(pair[:, 1].reshape(half * 8, states), powers[level])
        ups.append(pair[:, 0] + later.reshape(half, 8, states))

    last = jnp.zeros((8, states), F32)
    for b in range(seqs):
        r = (WORD - 1) * total + (b + 1) * chunks - 1
        last = jnp.where(row8 == b, jnp.broadcast_to(filt[r : r + 1, :], (8, states)), last)
    final = times(last, stacked(d_t))
    own = ups[-1][0] + jnp.where(pos == n - 1, times(final, powers[levels]), 0.0)
    off_buf[...] = own

    def send_off(d):
        return pltpu.make_async_remote_copy(
            src_ref=off_buf, dst_ref=off_in.at[d], send_sem=off_send.at[d], recv_sem=off_recv.at[d],
            device_id={"tm": lax.rem(pos + n - 1 - d, n)}, device_id_type=MESH,
        )

    for d in range(n - 1):
        @pl.when(pos - 1 - d >= 0)
        def _(d=d):
            send_off(d).start()

    obs_rows = [at(obs, i) for i in range(WORD)]
    mask_rows = [at(mask, i) for i in range(WORD)]
    errors = jnp.concatenate(obs_rows, axis=0) - times(prior[...], stacked(readout))
    seen = jnp.concatenate(mask_rows, axis=0)
    squares = jnp.sum(seen * active * errors * errors, axis=0, keepdims=True)
    number = jnp.sum(seen, axis=0, keepdims=True)
    sums = jnp.where(row8 == 0, jnp.broadcast_to(squares, (8, states)), jnp.broadcast_to(number, (8, states)))
    sum_buf[...] = sums

    def send_sum(d):
        return pltpu.make_async_remote_copy(
            src_ref=sum_buf, dst_ref=sum_in.at[d], send_sem=sum_send.at[d], recv_sem=sum_recv.at[d],
            device_id={"tm": lax.rem(pos + d + 1, n)}, device_id_type=MESH,
        )

    for d in range(n - 1):
        send_sum(d).start()

    for d in range(n - 1):
        @pl.when(pos + 1 + d < n)
        def _(d=d):
            send_off(d).wait_recv()

    x = off_in[...]
    for power in laps:
        pair = x.reshape(x.shape[0] // 2, 2, 8, states)
        half = pair.shape[0]
        x = pair[:, 0] + times(pair[:, 1].reshape(half * 8, states), power).reshape(half, 8, states)
    x = jnp.where(pos == n - 1, final, x[0])[None]
    for level in range(levels - 1, -1, -1):
        count = x.shape[0]
        pair = ups[level].reshape(count, 2, 8, states)
        early = times(x.reshape(count * 8, states), powers[level]).reshape(count, 8, states) + pair[:, 1]
        x = jnp.stack([early, x], axis=1).reshape(2 * count, 8, states)
    chunk8[...] = x.reshape(chunks * 8, states)
    x = jnp.concatenate([chunk8[pl.ds(b, chunks, stride=8), :] for b in range(seqs)], axis=0)
    y = times(x, fill_rhs)
    for i in range(WORD):
        out[pl.ds(i, total, stride=WORD), :] = (
            suffix[i * total : (i + 1) * total, :] + y[:, i * states : (i + 1) * states]
        )

    for d in range(n - 1):
        send_sum(d).wait_recv()
        sums = sums + sum_in[d]
    squares, number = sums[0:1], sums[1:2]
    grad = 0.5 * active * (number - weight * squares)
    new_prec[...] = log_prec[...] + grad / (seqs * steps * n)
    terms = 0.5 * active * (log_prec[...] * number - weight * squares)
    loglik[...] = jnp.sum(terms, axis=1, keepdims=True) / (seqs * steps * n * states)

    @pl.when(pos < n - 1)
    def _():
        chain.wait_send()

    for d in range(n - 1):
        @pl.when(pos - 1 - d >= 0)
        def _(d=d):
            send_off(d).wait_send()
        send_sum(d).wait_send()


def local(n, obs, present, sensors, log_prec, dynamics, prior_var, obs_map, init_state):
    seqs, steps, channels = obs.shape
    states = dynamics.shape[0]
    chunks = steps // WORD
    total = seqs * chunks
    inner = sum(total >> level for level in range(1, int(math.log2(chunks)) + 1))
    ents = sum((((total >> level) + 7) // 8) * 8 for level in range(0, int(math.log2(chunks)) + 1))
    vmem = pl.BlockSpec(memory_space=pltpu.VMEM)
    smem = pl.BlockSpec(memory_space=pltpu.SMEM)
    rows = seqs * steps
    smoothed, new_prec, loglik = pl.pallas_call(
        functools.partial(kernel, n, seqs, steps),
        out_shape=(
            jax.ShapeDtypeStruct((rows, states), F32),
            jax.ShapeDtypeStruct((1, channels), F32),
            jax.ShapeDtypeStruct((1, 1), F32),
        ),
        in_specs=[smem, smem] + [vmem] * 7,
        out_specs=(vmem, vmem, vmem),
        scratch_shapes=[
            pltpu.SMEM((total,), jnp.int32),
            pltpu.VMEM((2**WORD, 2 * states, states), BF16),
            pltpu.VMEM((inner, 2 * states, states), BF16),
            pltpu.VMEM(((inner + 7) // 8 * 8, states), F32),
            pltpu.VMEM((ents, states), F32),
            pltpu.VMEM((2 * states, 4 * states), BF16),
            pltpu.VMEM((2 * states, 2 * states), BF16),
            pltpu.VMEM((rows, states), F32),
            pltpu.VMEM((rows, states), F32),
            pltpu.VMEM((total, states), F32),
            pltpu.VMEM((rows, states), F32),
            pltpu.VMEM((rows, states), F32),
            pltpu.VMEM((rows, states), F32),
            pltpu.VMEM((chunks * 8, states), F32),
            pltpu.VMEM((8, states), F32),
            pltpu.VMEM((8, states), F32),
            pltpu.VMEM((8, states), F32),
            pltpu.VMEM((n, 8, states), F32),
            pltpu.VMEM((8, states), F32),
            pltpu.VMEM((n, 8, states), F32),
            pltpu.SemaphoreType.DMA((2,)),
            pltpu.SemaphoreType.DMA((n,)),
            pltpu.SemaphoreType.DMA((n,)),
            pltpu.SemaphoreType.DMA((n,)),
            pltpu.SemaphoreType.DMA((n,)),
        ],
        compiler_params=pltpu.CompilerParams(collective_id=0, has_side_effects=True),
        name="kalman",
    )(
        present, sensors, obs.reshape(rows, channels), present, log_prec.reshape(1, channels),
        dynamics, prior_var.reshape(1, states), obs_map, init_state,
    )
    return smoothed.reshape(seqs, steps, states), new_prec.reshape(channels), loglik.reshape(1)


def solution(mesh):
    in_specs = (
        P("cluster", "tm", None),
        P("cluster", "tm"),
        P("cluster"),
        P("cluster"),
        P("cluster", None),
        P("cluster"),
        P("cluster", None),
        P("cluster", None),
    )
    out_specs = (P("cluster", "tm", None), P("cluster"), P("cluster"))
    body = functools.partial(local, mesh.shape["tm"])
    return jax.shard_map(body, mesh=mesh, in_specs=in_specs, out_specs=out_specs, check_vma=False)
```

profile of v0, /device:TPU:8, one launch (start us, length us, event | category | flops | bytes accessed | tf_op | source)
XLA Modules:
  0.0 36.1 jit_solution(5187386120085704799)
XLA Ops:
  1.3 30.9 %kalman.1 = (f32[192,128]{1,0:T(8,128)}, f32[1,128]{1,0:T(1,128)}, f32[1,1]{1,0:T(1,128)}) custom-call(s32[3,64]{1,0:T(4,128)} %present_v.1, s32[1]{0:T(128)S(6)} %copy.14.sensors_s, f32[192,128]{1,0:T(8,128)} %bitcast.7, s32[3,64]{1,0:T(4,128)} %present_v.1, f32[1,128]{1,0:T(1,128)} %bitcast.8, f32[128,128]{1,0:T(8,128)} %dyn.1, f32[1,128]{1,0:T(1,128)} %bitcast.9, ...), custom_call_target="tpu_custom_call" | custom-call | tf_op jit(solution)/shard_map/kalman/pallas_call | solution.py:333
  32.2 0.0 copy-start
  32.2 1.5 %copy.15 = f32[3,64,128]{2,1,0:T(8,128)} copy(f32[3,64,128]{2,1,0:T(8,128)} %bitcast.6) | data formatting | bytes 196608
  33.7 0.0 copy-done
  33.7 0.5 %copy.16 = f32[128]{0:T(128)} copy(f32[128]{0:T(128)S(1)} %bitcast.10) | data formatting | bytes 1024
Async XLA Ops:
  32.2 1.6 %copy-start = (f32[1,128]{1,0:T(1,128)S(1)}, f32[1,128]{1,0:T(1,128)}, u32[]{:S(2)}) copy-start(f32[1,128]{1,0:T(1,128)} %get-tuple-element.7) | copy-start | bytes 1540
where the time goes:
time: 36.3 us; the launch traced here: 36.1 us
  Pallas kernels  30.9 us (85%)
  between operations  3.11 us (9%)
  local copies, waits for them, and re-layouts  2.06 us (6%)
    pallas_call x1, Pallas kernels, local(): pl.pallas_call(functools.partial(kernel, n, seqs, steps), out_shape=(jax....  30.9 us
    unnamed x4, local copies, waits for them, and re-layouts  2.06 us

commit v1 on v0

--- a/solution.py
+++ b/solution.py
@@ -52,7 +52,7 @@
     n, seqs, steps,
     present_s, sensors_s, obs, present_v, log_prec, dyn, prior_var, obs_map, init,
     out, new_prec, loglik,
-    words, table, nodes, vecs, ents, pair_rhs, step_rhs, drive, mask, offs, prior, filt,
+    words, table, nodes, vecs, ents, heads, head_vecs, power_rows, power_cols, lap_rhs, pair_rhs, step_rhs, drive, mask, offs, prior, filt,
     suffix, chunk8, in_buf, out_buf, off_buf, off_in, sum_buf, sum_in,
     chain_sem, off_send, off_recv, sum_send, sum_recv,
 ):
@@ -127,7 +127,7 @@
         lax.broadcasted_iota(jnp.int32, (states, states), 0)
         == lax.broadcasted_iota(jnp.int32, (states, states), 1)
     ).astype(F32)
-    residual = eye - jnp.dot(d_t, d_mat, precision=lax.Precision.HIGHEST, preferred_element_type=F32)
+    residual = eye - times(d_t, d_rhs)
     by_one = times(jnp.concatenate([residual, d_mat], axis=0), d_rhs)
     r_1, d_2 = by_one[:states], by_one[states:]
     by_two = times(jnp.concatenate([residual, r_1, d_mat, d_2], axis=0), stacked(d_2))
@@ -135,8 +135,19 @@
     d_3, d_4 = by_two[2 * states : 3 * states], by_two[3 * states :]
     tail_rhs = stacked(jnp.concatenate([residual, r_1, r_2, r_3], axis=1))
     fill_rhs = stacked(jnp.concatenate([d_4, d_3, d_2, d_mat], axis=1))
-    power = stacked(d_4)
-    powers = [power]
+
+    def keep_power(e, stack):
+        if e < chunks:
+            power_rows[e * 2 * states : (e + 1) * 2 * states, :] = stack
+            power_cols[:, (chunks - 1 - e) * states : (chunks - e) * states] = stack
+        else:
+            lap_rhs[0 : 2 * states, :] = stack
+
+    def power_of(e):
+        return power_rows[e * 2 * states : (e + 1) * 2 * states, :]
+
+    keep_power(0, stacked(eye))
+    keep_power(1, stacked(d_4))
 
     for level in range(1, levels + 1):
         base, below = first[level], first[level - 1]
@@ -155,13 +166,54 @@
                 y[2 * states : 2 * states + 1] + y[2 * states + 8 : 2 * states + 9] + v_right
             )
 
-        over(total >> level, 6, compose)
-        power = stacked(product(twice(powers[-1]), powers[-1]))
-        powers.append(power)
-    laps = []
-    for _ in range(int(math.log2(n))):
-        laps.append(power)
-        power = stacked(product(twice(power), power))
+        over(total >> level, total, compose)
+        half = power_of(1 << (level - 1))
+        keep_power(1 << level, stacked(product(twice(half), half)))
+
+    def prepare():
+        for b in range(seqs):
+            rows = slice(b * 2 * states, (b + 1) * 2 * states)
+            heads[rows, 0:states] = stacked(eye)
+            for level in range(levels, 0, -1):
+                for p in range(chunks >> level):
+                    j = b * (chunks >> (level - 1)) + 2 * p
+                    k = (p << level) + (1 << (level - 1))
+                    if level == 1:
+                        mat, v = table[words[j]], offs[j : j + 1, :]
+                    else:
+                        j = first[level - 1] + j
+                        mat, v = nodes[j], vecs[j : j + 1, :]
+                    if p > 0:
+                        before = p << level
+                        e_rows = head_vecs[b * chunks + before : b * chunks + before + 1, :]
+                        left = jnp.concatenate(
+                            [heads[rows, before * states : (before + 1) * states],
+                             stacked(jnp.broadcast_to(e_rows, (8, states)))], axis=0)
+                        y = jnp.dot(twice(left), mat, preferred_element_type=F32)
+                        mat = stacked(y[:states] + y[states : 2 * states])
+                        v = y[2 * states : 2 * states + 1] + y[2 * states + 8 : 2 * states + 9] + v
+                    heads[rows, k * states : (k + 1) * states] = mat
+                    head_vecs[b * chunks + k : b * chunks + k + 1, :] = v
+        for level in range(1, levels):
+            base = power_of(1 << level)
+            for e in range(1, 1 << level):
+                keep_power((1 << level) + e, stacked(product(twice(power_of(e)), base)))
+        for d in range(1, n - 2):
+            half = (d + 1) // 2 - 1
+            other = d - 1 - half
+            lap_rhs[d * 2 * states : (d + 1) * 2 * states, :] = stacked(
+                product(
+                    twice(lap_rhs[half * 2 * states : (half + 1) * 2 * states, :]),
+                    lap_rhs[other * 2 * states : (other + 1) * 2 * states, :],
+                )
+            )
+
+    head_vecs[...] = jnp.zeros_like(head_vecs)
+    early = n // 2
+
+    @pl.when(pos >= early)
+    def _():
+        prepare()
 
     pl.semaphore_wait(barrier, n - 1)
     row8 = lax.broadcasted_iota(jnp.int32, (8, states), 0)
@@ -181,37 +233,26 @@
 
     entering = in_buf[...]
     top = first[levels]
-    left = twice(stacked(entering))
+    left = jnp.concatenate(
+        [twice(stacked(jnp.where(row8 == b, entering, 0.0))) for b in range(seqs)], axis=1
+    )
 
     @pl.when(pos < n - 1)
     def _():
-        leaving = jnp.zeros((8, states), F32)
+        leaving = product(left, nodes[top : top + seqs].reshape(seqs * 2 * states, states))
         for b in range(seqs):
-            y = product(left, nodes[top + b]) + vecs[top + b : top + b + 1, :]
-            leaving = jnp.where(row8 == b, y, leaving)
+            leaving = leaving + jnp.where(row8 == b, vecs[top + b : top + b + 1, :], 0.0)
         out_buf[...] = leaving
         chain.start()
 
-    e_first = [0]
-    for level in range(levels, 0, -1):
-        e_first.append(e_first[-1] + (((total >> level) + 7) // 8) * 8)
-    ents[0:seqs, :] = entering[0:seqs]
-    for lap, level in enumerate(range(levels, 0, -1)):
-        source, target, below = e_first[lap], e_first[lap + 1], first[level - 1]
-
-        def descend(j, level=level, source=source, target=target, below=below):
-            e = ents[pl.ds(source + j, 1), :]
-            if level == 1:
-                mat, v = table[words[2 * j]], offs[pl.ds(2 * j, 1), :]
-            else:
-                mat, v = nodes[below + 2 * j], vecs[pl.ds(below + 2 * j, 1), :]
-            y = times(jnp.broadcast_to(e, (8, states)), mat)
-            ents[pl.ds(target + 2 * j, 1), :] = e
-            ents[pl.ds(target + 2 * j + 1, 1), :] = y[0:1] + v
-
-        over(total >> level, 6, descend)
-
-    x = ents[pl.ds(e_first[-1], total), :]
+    @pl.when(pos < early)
+    def _():
+        prepare()
+
+    y = product(left, heads[...])
+    for k in range(chunks):
+        ents[pl.ds(k, seqs, stride=chunks), :] = y[0:seqs, k * states : (k + 1) * states]
+    x = ents[...] + head_vecs[...]
     for i in range(WORD):
         prior[i * total : (i + 1) * total, :] = x
         x = advance(x, i)
@@ -232,19 +273,15 @@
             for b in range(seqs):
                 chunk8[pl.ds(b, chunks, stride=8), :] = z[b * chunks : (b + 1) * chunks]
 
-    ups = [chunk8[...].reshape(chunks, 8, states)]
-    for level in range(levels):
-        pair = ups[-1].reshape(ups[-1].shape[0] // 2, 2, 8, states)
-        half = pair.shape[0]
-        later = times(pair[:, 1].reshape(half * 8, states), powers[level])
-        ups.append(pair[:, 0] + later.reshape(half, 8, states))
-
     last = jnp.zeros((8, states), F32)
     for b in range(seqs):
         r = (WORD - 1) * total + (b + 1) * chunks - 1
         last = jnp.where(row8 == b, jnp.broadcast_to(filt[r : r + 1, :], (8, states)), last)
     final = times(last, stacked(d_t))
-    own = ups[-1][0] + jnp.where(pos == n - 1, times(final, powers[levels]), 0.0)
+    ends = chunk8[...].reshape(chunks, 8, states)
+    left = jnp.concatenate([twice(stacked(ends[k])) for k in range(chunks)], axis=1)
+    own = product(left, power_rows[...])
+    own = own + jnp.where(pos == n - 1, times(final, lap_rhs[0 : 2 * states, :]), 0.0)
     off_buf[...] = own
 
     def send_off(d):
@@ -276,23 +313,34 @@
     for d in range(n - 1):
         send_sum(d).start()
 
+    ups = [ends]
+    for level in range(levels):
+        pair = ups[-1].reshape(ups[-1].shape[0] // 2, 2, 8, states)
+        half = pair.shape[0]
+        later = times(pair[:, 1].reshape(half * 8, states), power_of(1 << level))
+        ups.append(pair[:, 0] + later.reshape(half, 8, states))
+    x = jnp.zeros((1, 8, states), F32)
+    for level in range(levels - 1, -1, -1):
+        count = x.shape[0]
+        pair = ups[level].reshape(count, 2, 8, states)
+        if level == levels - 1:
+            sooner = pair[:, 1]
+        else:
+            moved = times(x.reshape(count * 8, states), power_of(1 << level))
+            sooner = moved.reshape(count, 8, states) + pair[:, 1]
+        x = jnp.stack([sooner, x], axis=1).reshape(2 * count, 8, states)
+    chunk8[...] = x.reshape(chunks * 8, states)
+
     for d in range(n - 1):
         @pl.when(pos + 1 + d < n)
         def _(d=d):
             send_off(d).wait_recv()
 
-    x = off_in[...]
-    for power in laps:
-        pair = x.reshape(x.shape[0] // 2, 2, 8, states)
-        half = pair.shape[0]
-        x = pair[:, 0] + times(pair[:, 1].reshape(half * 8, states), power).reshape(half, 8, states)
-    x = jnp.where(pos == n - 1, final, x[0])[None]
-    for level in range(levels - 1, -1, -1):
-        count = x.shape[0]
-        pair = ups[level].reshape(count, 2, 8, states)
-        early = times(x.reshape(count * 8, states), powers[level]).reshape(count, 8, states) + pair[:, 1]
-        x = jnp.stack([early, x], axis=1).reshape(2 * count, 8, states)
-    chunk8[...] = x.reshape(chunks * 8, states)
+    left = jnp.concatenate([twice(stacked(off_in[d])) for d in range(1, n - 1)], axis=1)
+    x = jnp.where(pos == n - 1, final, off_in[0] + product(left, lap_rhs[...]))
+    y = times(x, power_cols[...])
+    for k in range(chunks):
+        chunk8[k * 8 : (k + 1) * 8, :] += y[:, k * states : (k + 1) * states]
     x = jnp.concatenate([chunk8[pl.ds(b, chunks, stride=8), :] for b in range(seqs)], axis=0)
     y = times(x, fill_rhs)
     for i in range(WORD):
@@ -326,7 +374,6 @@
     chunks = steps // WORD
     total = seqs * chunks
     inner = sum(total >> level for level in range(1, int(math.log2(chunks)) + 1))
-    ents = sum((((total >> level) + 7) // 8) * 8 for level in range(0, int(math.log2(chunks)) + 1))
     vmem = pl.BlockSpec(memory_space=pltpu.VMEM)
     smem = pl.BlockSpec(memory_space=pltpu.SMEM)
     rows = seqs * steps
@@ -344,7 +391,12 @@
             pltpu.VMEM((2**WORD, 2 * states, states), BF16),
             pltpu.VMEM((inner, 2 * states, states), BF16),
             pltpu.VMEM(((inner + 7) // 8 * 8, states), F32),
-            pltpu.VMEM((ents, states), F32),
+            pltpu.VMEM((total, states), F32),
+            pltpu.VMEM((seqs * 2 * states, chunks * states), BF16),
+            pltpu.VMEM((total, states), F32),
+            pltpu.VMEM((chunks * 2 * states, states), BF16),
+            pltpu.VMEM((2 * states, chunks * states), BF16),
+            pltpu.VMEM(((n - 2) * 2 * states, states), BF16),
             pltpu.VMEM((2 * states, 4 * states), BF16),
             pltpu.VMEM((2 * states, 2 * states), BF16),
             pltpu.VMEM((rows, states), F32),

time: 36.3 us -> 27.9 us (0.77)
  Pallas kernels: 30.9 us -> 22.4 us
    pallas_call x1, Pallas kernels: 30.9 us -> 22.4 us  [local(): pl.pallas_call(functools.partial(kernel, n, seqs, steps), out_shape=(jax....]
where the time goes in v1:
time: 27.9 us; the launch traced here: 27.5 us
  Pallas kernels  22.4 us (80%)
  between operations  3.11 us (11%)
  local copies, waits for them, and re-layouts  2.06 us (7%)
    pallas_call x1, Pallas kernels, local(): pl.pallas_call(functools.partial(kernel, n, seqs, steps), out_shape=(jax....  22.4 us
    unnamed x4, local copies, waits for them, and re-layouts  2.06 us

profile of v1, /device:TPU:8, one launch (start us, length us, event | category | flops | bytes accessed | tf_op | source)
XLA Modules:
  0.0 27.5 jit_solution(7914782801478040894)
XLA Ops:
  1.3 22.4 %kalman.1 = (f32[192,128]{1,0:T(8,128)}, f32[1,128]{1,0:T(1,128)}, f32[1,1]{1,0:T(1,128)}) custom-call(s32[3,64]{1,0:T(4,128)} %present_v.1, s32[1]{0:T(128)S(6)} %copy.14.sensors_s, f32[192,128]{1,0:T(8,128)} %bitcast.7, s32[3,64]{1,0:T(4,128)} %present_v.1, f32[1,128]{1,0:T(1,128)} %bitcast.8, f32[128,128]{1,0:T(8,128)} %dyn.1, f32[1,128]{1,0:T(1,128)} %bitcast.9, ...), custom_call_target="tpu_custom_call" | custom-call | tf_op jit(solution)/shard_map/kalman/pallas_call | solution.py:380
  23.6 0.0 copy-start
  23.7 1.5 %copy.15 = f32[3,64,128]{2,1,0:T(8,128)} copy(f32[3,64,128]{2,1,0:T(8,128)} %bitcast.6) | data formatting | bytes 196608
  25.2 0.0 copy-done
  25.2 0.5 %copy.16 = f32[128]{0:T(128)} copy(f32[128]{0:T(128)S(1)} %bitcast.10) | data formatting | bytes 1024
Async XLA Ops:
  23.6 1.6 %copy-start = (f32[1,128]{1,0:T(1,128)S(1)}, f32[1,128]{1,0:T(1,128)}, u32[]{:S(2)}) copy-start(f32[1,128]{1,0:T(1,128)} %get-tuple-element.7) | copy-start | bytes 1540
